TPU v7x, 256 devices: a whole 4x4x8 slice. The times are simulated.
256 devices in a mesh: pairs: 32 (over z, y_hi, core), aux: 8 (over x, y_lo).
Axes of the slice: x: 4, y: 4 (y_hi: 2, y_lo: 2; y = y_hi * 2 + y_lo), z: 8, core: 2. Of those that a mesh axis runs over, the one named last changes fastest.
Arguments:
- amplitudes: float32 [64, 256, 256], P('pairs'), may hold values from -6 to 6
- factors: float32 [384, 256, 256], P('aux', 'pairs'), may hold values from -0.078125 to 0.078125
- occ_factors: float32 [384, 8, 8], P('aux'), may hold values from -0.5 to 0.5
Outputs:
- resid: float32 [64, 256, 256], P(None, 'pairs', 'aux')
All inputs are finite; a program needn't handle non-finite values.
Results may differ from a plain program's by a relative error of at most 0.0001.
Values sent between devices are 32-bit elements; how exact they have to be, the bound alone decides.
A program may use at most 64 MiB of HBM per device.

v0:
```python
import jax
import jax.numpy as jnp
from jax import lax
from jax.sharding import PartitionSpec as P

highest = lax.Precision.HIGHEST


def both_sides(running, amps, row_block):
    mixed_terms = jnp.einsum("icd,pbd->picb", amps, row_block, precision=highest)
    return running + jnp.einsum("pac,picb->iab", row_block, mixed_terms, precision=highest)


def shards(amplitudes, factors, occ_factors):
    local_pairs = amplitudes.shape[0]
    virt_width = amplitudes.shape[1]
    aux_local = factors.shape[0]
    occupied = occ_factors.shape[1]
    total_pairs = occupied * occupied
    aux_rank = lax.axis_index("aux")
    column_count = virt_width // lax.axis_size("aux")
    col_start = aux_rank * column_count
    amp_cols = lax.dynamic_slice_in_dim(amplitudes, col_start, column_count, 2)
    amp_flip = jnp.swapaxes(lax.dynamic_slice_in_dim(amplitudes, col_start, column_count, 1), 1, 2)

    def whole_step(running, block_index):
        row_block = lax.dynamic_slice_in_dim(factors, block_index * 2, 2, 0)
        whole_rows = lax.all_gather(row_block, "pairs", axis=1, tiled=True)
        return (both_sides(running, amplitudes, whole_rows), None)

    particle, unused = lax.scan(
        whole_step,
        jnp.zeros((local_pairs, virt_width, virt_width), jnp.float32),
        jnp.arange(aux_local // 2),
    )
    coupling = jnp.einsum("pik,pjl->ijkl", occ_factors, occ_factors, precision=highest).reshape(
        total_pairs, total_pairs
    )
    particle, coupling = lax.psum((particle, coupling), "aux")
    part_cols = lax.dynamic_slice_in_dim(particle, col_start, column_count, 2)
    part_flip = jnp.swapaxes(lax.dynamic_slice_in_dim(particle, col_start, column_count, 1), 1, 2)
    part_cols, part_flip, amp_cols, amp_flip = (
        lax.all_to_all(part_cols, "pairs", split_axis=1, concat_axis=0, tiled=True),
        lax.all_to_all(part_flip, "pairs", split_axis=1, concat_axis=0, tiled=True),
        lax.all_to_all(amp_cols, "pairs", split_axis=1, concat_axis=0, tiled=True),
        lax.all_to_all(amp_flip, "pairs", split_axis=1, concat_axis=0, tiled=True),
    )
    straight = part_cols + jnp.einsum("pk,kab->pab", coupling, amp_cols, precision=highest)
    turned = part_flip + jnp.einsum("pk,kab->pab", coupling, amp_flip, precision=highest)
    rows_here = turned.shape[1]
    turned = (
        turned.reshape(occupied, occupied, rows_here, column_count)
        .transpose(1, 0, 2, 3)
        .reshape(total_pairs, rows_here, column_count)
    )
    return straight + turned


def solution(mesh):
    placed = (P("pairs", None, None), P("aux", "pairs", None), P("aux", None, None))
    return jax.shard_map(
        shards, mesh=mesh, in_specs=placed, out_specs=P(None, "pairs", "aux"), check_vma=False
    )
```

profile of v0, /device:TPU:1, one launch (start us, length us, event | category | flops | bytes accessed | tf_op | source)
XLA Modules:
  0.0 1193.5 jit_solution(1170505517774073015)
XLA Ops:
  6.5 1064.0 %while.11 = (s32[]{:T(128)}, f32[2,256,256]{1,2,0:T(8,128)S(1)}, s32[24]{0:T(128)S(1)}, f32[48,8,256]{2,1,0:T(8,128)}, f32[2,256,256]{2,1,0:T(8,128)}, /*index=5*/s32[]{:T(128)}, s32[1]{0:T(128)}, s32[]{:T(128)}, s32[]{:T(128)}) while((s32[]{:T(128)}, f32[2,256,256]{1,2,0:T(8,128)S(1)}, s32[24]{0:T(128)S(1)}, ...), condition=%wide.region_1.2_spmd.clone, body=%wide.region_0.1_spmd.clone.sunk | while | flops 1610874880 | bytes 7389385 | solution.py:31
  8.6 47.7 %all_gather.5 = f32[2,256,256]{2,1,0:T(8,128)S(1)} all-gather(f32[2,8,256]{2,1,0:T(8,128)S(1)} %constant_dynamic-slice_fusion.5), channel_id=1, replica_groups=mesh['pairs'=32,'aux'=8] {'pairs'}, dimensions={1}, use_global_device_ids=true | all-gather | bytes 540672 | tf_op jit(solution)/shard_map/while/body/eval_jaxpr/all_gather | solution.py:28
  57.4 1.3 fusion.23
  60.8 38.1 %all_gather.5 = f32[2,256,256]{2,1,0:T(8,128)S(1)} all-gather(f32[2,8,256]{2,1,0:T(8,128)S(1)} %constant_dynamic-slice_fusion.5), channel_id=1, replica_groups=mesh['pairs'=32,'aux'=8] {'pairs'}, dimensions={1}, use_global_device_ids=true | all-gather | bytes 540672 | tf_op jit(solution)/shard_map/while/body/eval_jaxpr/all_gather | solution.py:28
  100.0 1.3 fusion.23
  103.3 41.1 %all_gather.5 = f32[2,256,256]{2,1,0:T(8,128)S(1)} all-gather(f32[2,8,256]{2,1,0:T(8,128)S(1)} %constant_dynamic-slice_fusion.5), channel_id=1, replica_groups=mesh['pairs'=32,'aux'=8] {'pairs'}, dimensions={1}, use_global_device_ids=true | all-gather | bytes 540672 | tf_op jit(solution)/shard_map/while/body/eval_jaxpr/all_gather | solution.py:28
  145.5 1.3 fusion.23
  148.9 38.1 %all_gather.5 = f32[2,256,256]{2,1,0:T(8,128)S(1)} all-gather(f32[2,8,256]{2,1,0:T(8,128)S(1)} %constant_dynamic-slice_fusion.5), channel_id=1, replica_groups=mesh['pairs'=32,'aux'=8] {'pairs'}, dimensions={1}, use_global_device_ids=true | all-gather | bytes 540672 | tf_op jit(solution)/shard_map/while/body/eval_jaxpr/all_gather | solution.py:28
  188.1 1.3 fusion.23
  191.5 41.1 %all_gather.5 = f32[2,256,256]{2,1,0:T(8,128)S(1)} all-gather(f32[2,8,256]{2,1,0:T(8,128)S(1)} %constant_dynamic-slice_fusion.5), channel_id=1, replica_groups=mesh['pairs'=32,'aux'=8] {'pairs'}, dimensions={1}, use_global_device_ids=true | all-gather | bytes 540672 | tf_op jit(solution)/shard_map/while/body/eval_jaxpr/all_gather | solution.py:28
  237.0 38.1 %all_gather.5 = f32[2,256,256]{2,1,0:T(8,128)S(1)} all-gather(f32[2,8,256]{2,1,0:T(8,128)S(1)} %constant_dynamic-slice_fusion.5), channel_id=1, replica_groups=mesh['pairs'=32,'aux'=8] {'pairs'}, dimensions={1}, use_global_device_ids=true | all-gather | bytes 540672 | tf_op jit(solution)/shard_map/while/body/eval_jaxpr/all_gather | solution.py:28
  276.2 1.3 fusion.23
  279.6 41.1 %all_gather.5 = f32[2,256,256]{2,1,0:T(8,128)S(1)} all-gather(f32[2,8,256]{2,1,0:T(8,128)S(1)} %constant_dynamic-slice_fusion.5), channel_id=1, replica_groups=mesh['pairs'=32,'aux'=8] {'pairs'}, dimensions={1}, use_global_device_ids=true | all-gather | bytes 540672 | tf_op jit(solution)/shard_map/while/body/eval_jaxpr/all_gather | solution.py:28
  325.1 38.1 %all_gather.5 = f32[2,256,256]{2,1,0:T(8,128)S(1)} all-gather(f32[2,8,256]{2,1,0:T(8,128)S(1)} %constant_dynamic-slice_fusion.5), channel_id=1, replica_groups=mesh['pairs'=32,'aux'=8] {'pairs'}, dimensions={1}, use_global_device_ids=true | all-gather | bytes 540672 | tf_op jit(solution)/shard_map/while/body/eval_jaxpr/all_gather | solution.py:28
  364.3 1.3 fusion.23
  367.7 41.1 %all_gather.5 = f32[2,256,256]{2,1,0:T(8,128)S(1)} all-gather(f32[2,8,256]{2,1,0:T(8,128)S(1)} %constant_dynamic-slice_fusion.5), channel_id=1, replica_groups=mesh['pairs'=32,'aux'=8] {'pairs'}, dimensions={1}, use_global_device_ids=true | all-gather | bytes 540672 | tf_op jit(solution)/shard_map/while/body/eval_jaxpr/all_gather | solution.py:28
  413.3 38.1 %all_gather.5 = f32[2,256,256]{2,1,0:T(8,128)S(1)} all-gather(f32[2,8,256]{2,1,0:T(8,128)S(1)} %constant_dynamic-slice_fusion.5), channel_id=1, replica_groups=mesh['pairs'=32,'aux'=8] {'pairs'}, dimensions={1}, use_global_device_ids=true | all-gather | bytes 540672 | tf_op jit(solution)/shard_map/while/body/eval_jaxpr/all_gather | solution.py:28
  452.4 1.3 fusion.23
  455.8 41.1 %all_gather.5 = f32[2,256,256]{2,1,0:T(8,128)S(1)} all-gather(f32[2,8,256]{2,1,0:T(8,128)S(1)} %constant_dynamic-slice_fusion.5), channel_id=1, replica_groups=mesh['pairs'=32,'aux'=8] {'pairs'}, dimensions={1}, use_global_device_ids=true | all-gather | bytes 540672 | tf_op jit(solution)/shard_map/while/body/eval_jaxpr/all_gather | solution.py:28
  501.4 38.1 %all_gather.5 = f32[2,256,256]{2,1,0:T(8,128)S(1)} all-gather(f32[2,8,256]{2,1,0:T(8,128)S(1)} %constant_dynamic-slice_fusion.5), channel_id=1, replica_groups=mesh['pairs'=32,'aux'=8] {'pairs'}, dimensions={1}, use_global_device_ids=true | all-gather | bytes 540672 | tf_op jit(solution)/shard_map/while/body/eval_jaxpr/all_gather | solution.py:28
  540.5 1.3 fusion.23
  543.9 41.1 %all_gather.5 = f32[2,256,256]{2,1,0:T(8,128)S(1)} all-gather(f32[2,8,256]{2,1,0:T(8,128)S(1)} %constant_dynamic-slice_fusion.5), channel_id=1, replica_groups=mesh['pairs'=32,'aux'=8] {'pairs'}, dimensions={1}, use_global_device_ids=true | all-gather | bytes 540672 | tf_op jit(solution)/shard_map/while/body/eval_jaxpr/all_gather | solution.py:28
  589.5 38.1 %all_gather.5 = f32[2,256,256]{2,1,0:T(8,128)S(1)} all-gather(f32[2,8,256]{2,1,0:T(8,128)S(1)} %constant_dynamic-slice_fusion.5), channel_id=1, replica_groups=mesh['pairs'=32,'aux'=8] {'pairs'}, dimensions={1}, use_global_device_ids=true | all-gather | bytes 540672 | tf_op jit(solution)/shard_map/while/body/eval_jaxpr/all_gather | solution.py:28
  628.7 1.3 fusion.23
  632.1 41.1 %all_gather.5 = f32[2,256,256]{2,1,0:T(8,128)S(1)} all-gather(f32[2,8,256]{2,1,0:T(8,128)S(1)} %constant_dynamic-slice_fusion.5), channel_id=1, replica_groups=mesh['pairs'=32,'aux'=8] {'pairs'}, dimensions={1}, use_global_device_ids=true | all-gather | bytes 540672 | tf_op jit(solution)/shard_map/while/body/eval_jaxpr/all_gather | solution.py:28
  677.6 38.1 %all_gather.5 = f32[2,256,256]{2,1,0:T(8,128)S(1)} all-gather(f32[2,8,256]{2,1,0:T(8,128)S(1)} %constant_dynamic-slice_fusion.5), channel_id=1, replica_groups=mesh['pairs'=32,'aux'=8] {'pairs'}, dimensions={1}, use_global_device_ids=true | all-gather | bytes 540672 | tf_op jit(solution)/shard_map/while/body/eval_jaxpr/all_gather | solution.py:28
  716.8 1.3 fusion.23
  720.2 41.1 %all_gather.5 = f32[2,256,256]{2,1,0:T(8,128)S(1)} all-gather(f32[2,8,256]{2,1,0:T(8,128)S(1)} %constant_dynamic-slice_fusion.5), channel_id=1, replica_groups=mesh['pairs'=32,'aux'=8] {'pairs'}, dimensions={1}, use_global_device_ids=true | all-gather | bytes 540672 | tf_op jit(solution)/shard_map/while/body/eval_jaxpr/all_gather | solution.py:28
  765.7 38.1 %all_gather.5 = f32[2,256,256]{2,1,0:T(8,128)S(1)} all-gather(f32[2,8,256]{2,1,0:T(8,128)S(1)} %constant_dynamic-slice_fusion.5), channel_id=1, replica_groups=mesh['pairs'=32,'aux'=8] {'pairs'}, dimensions={1}, use_global_device_ids=true | all-gather | bytes 540672 | tf_op jit(solution)/shard_map/while/body/eval_jaxpr/all_gather | solution.py:28
  804.9 1.3 fusion.23
  808.3 41.1 %all_gather.5 = f32[2,256,256]{2,1,0:T(8,128)S(1)} all-gather(f32[2,8,256]{2,1,0:T(8,128)S(1)} %constant_dynamic-slice_fusion.5), channel_id=1, replica_groups=mesh['pairs'=32,'aux'=8] {'pairs'}, dimensions={1}, use_global_device_ids=true | all-gather | bytes 540672 | tf_op jit(solution)/shard_map/while/body/eval_jaxpr/all_gather | solution.py:28
  853.8 38.1 %all_gather.5 = f32[2,256,256]{2,1,0:T(8,128)S(1)} all-gather(f32[2,8,256]{2,1,0:T(8,128)S(1)} %constant_dynamic-slice_fusion.5), channel_id=1, replica_groups=mesh['pairs'=32,'aux'=8] {'pairs'}, dimensions={1}, use_global_device_ids=true | all-gather | bytes 540672 | tf_op jit(solution)/shard_map/while/body/eval_jaxpr/all_gather | solution.py:28
  893.0 1.3 fusion.23
  896.4 41.1 %all_gather.5 = f32[2,256,256]{2,1,0:T(8,128)S(1)} all-gather(f32[2,8,256]{2,1,0:T(8,128)S(1)} %constant_dynamic-slice_fusion.5), channel_id=1, replica_groups=mesh['pairs'=32,'aux'=8] {'pairs'}, dimensions={1}, use_global_device_ids=true | all-gather | bytes 540672 | tf_op jit(solution)/shard_map/while/body/eval_jaxpr/all_gather | solution.py:28
  942.0 38.1 %all_gather.5 = f32[2,256,256]{2,1,0:T(8,128)S(1)} all-gather(f32[2,8,256]{2,1,0:T(8,128)S(1)} %constant_dynamic-slice_fusion.5), channel_id=1, replica_groups=mesh['pairs'=32,'aux'=8] {'pairs'}, dimensions={1}, use_global_device_ids=true | all-gather | bytes 540672 | tf_op jit(solution)/shard_map/while/body/eval_jaxpr/all_gather | solution.py:28
  981.1 1.3 fusion.23
  984.5 41.1 %all_gather.5 = f32[2,256,256]{2,1,0:T(8,128)S(1)} all-gather(f32[2,8,256]{2,1,0:T(8,128)S(1)} %constant_dynamic-slice_fusion.5), channel_id=1, replica_groups=mesh['pairs'=32,'aux'=8] {'pairs'}, dimensions={1}, use_global_device_ids=true | all-gather | bytes 540672 | tf_op jit(solution)/shard_map/while/body/eval_jaxpr/all_gather | solution.py:28
  1030.1 38.1 %all_gather.5 = f32[2,256,256]{2,1,0:T(8,128)S(1)} all-gather(f32[2,8,256]{2,1,0:T(8,128)S(1)} %constant_dynamic-slice_fusion.5), channel_id=1, replica_groups=mesh['pairs'=32,'aux'=8] {'pairs'}, dimensions={1}, use_global_device_ids=true | all-gather | bytes 540672 | tf_op jit(solution)/shard_map/while/body/eval_jaxpr/all_gather | solution.py:28
  1069.3 1.3 fusion.23
  1073.7 6.1 all-to-all-start.3
  1082.0 7.6 all-to-all-done.3
  1089.6 3.9 all-to-all-start.1
  1093.5 26.1 %psum.15 = f32[64,64]{1,0:T(8,128)S(1)} all-reduce(f32[64,64]{1,0:T(8,128)S(1)} %reshape.11), channel_id=1, replica_groups=mesh['pairs'=32,'aux'=8] {'aux'}, use_global_device_ids=true, to_apply=%region_3.4 | all-reduce | flops 4096 | bytes 32768 | tf_op jit(solution)/shard_map/psum | solution.py:39
  1121.2 22.7 %all-reduce.2.cloned.1.call-done = f32[2,256,256]{2,0,1:T(2,128)} async-done(((f32[2,256,256]{2,0,1:T(2,128)}), f32[2,256,256]{2,0,1:T(2,128)}) %all-reduce.2.cloned.1.call-update) | async-done | bytes 524304 | tf_op jit(solution)/shard_map/psum | solution.py:39
  1145.9 15.2 %all-to-all-start.2 = ((f32[32,1,512]{2,1,0:T(1,128)}), f32[32,1,512]{2,1,0:T(1,128)S(1)}, u32[]{:S(2)}, u32[]{:S(2)}) async-start(f32[32,1,512]{2,1,0:T(1,128)} %reshape.22), calls=%async_computation.2 | async-start | bytes 131072 | tf_op jit(solution)/shard_map/all_to_all | solution.py:44
  1164.6 6.3 all-to-all-done.2
  1170.9 3.9 all-to-all-start
  1176.6 8.2 all-to-all-done
  (184 shorter events, 86.8 us)
Async XLA Ops:
  6.5 1073.3 %copy-start = (f32[48,8,8]{0,2,1:T(8,128)S(1)}, f32[48,8,8]{0,2,1:T(8,128)}, u32[]{:S(2)}) copy-start(f32[48,8,8]{0,2,1:T(8,128)} %param.7) | copy-start | bytes 36868
  6.5 1137.5 %all-reduce.2.cloned.1.call-start = ((), (), s32[]{:S(2)}) async-start(), calls=%async_computation.4 | async-start | bytes 1048576 | tf_op jit(solution)/shard_map/psum | solution.py:39
  6.5 49.8 %copy-start.1 = (f32[2,256,256]{2,1,0:T(8,128)S(1)}, f32[2,256,256]{2,1,0:T(8,128)}, u32[]{:S(2)}) copy-start(f32[2,256,256]{2,1,0:T(8,128)} %get-tuple-element.114) | copy-start | bytes 1572868 | tf_op jit(solution)/shard_map/while
  58.7 40.2 %copy-start.1 = (f32[2,256,256]{2,1,0:T(8,128)S(1)}, f32[2,256,256]{2,1,0:T(8,128)}, u32[]{:S(2)}) copy-start(f32[2,256,256]{2,1,0:T(8,128)} %get-tuple-element.114) | copy-start | bytes 1572868 | tf_op jit(solution)/shard_map/while
  101.2 43.2 %copy-start.1 = (f32[2,256,256]{2,1,0:T(8,128)S(1)}, f32[2,256,256]{2,1,0:T(8,128)}, u32[]{:S(2)}) copy-start(f32[2,256,256]{2,1,0:T(8,128)} %get-tuple-element.114) | copy-start | bytes 1572868 | tf_op jit(solution)/shard_map/while
  146.8 40.2 %copy-start.1 = (f32[2,256,256]{2,1,0:T(8,128)S(1)}, f32[2,256,256]{2,1,0:T(8,128)}, u32[]{:S(2)}) copy-start(f32[2,256,256]{2,1,0:T(8,128)} %get-tuple-element.114) | copy-start | bytes 1572868 | tf_op jit(solution)/shard_map/while
  189.4 43.2 %copy-start.1 = (f32[2,256,256]{2,1,0:T(8,128)S(1)}, f32[2,256,256]{2,1,0:T(8,128)}, u32[]{:S(2)}) copy-start(f32[2,256,256]{2,1,0:T(8,128)} %get-tuple-element.114) | copy-start | bytes 1572868 | tf_op jit(solution)/shard_map/while
  234.9 40.2 %copy-start.1 = (f32[2,256,256]{2,1,0:T(8,128)S(1)}, f32[2,256,256]{2,1,0:T(8,128)}, u32[]{:S(2)}) copy-start(f32[2,256,256]{2,1,0:T(8,128)} %get-tuple-element.114) | copy-start | bytes 1572868 | tf_op jit(solution)/shard_map/while
  277.5 43.2 %copy-start.1 = (f32[2,256,256]{2,1,0:T(8,128)S(1)}, f32[2,256,256]{2,1,0:T(8,128)}, u32[]{:S(2)}) copy-start(f32[2,256,256]{2,1,0:T(8,128)} %get-tuple-element.114) | copy-start | bytes 1572868 | tf_op jit(solution)/shard_map/while
  323.0 40.2 %copy-start.1 = (f32[2,256,256]{2,1,0:T(8,128)S(1)}, f32[2,256,256]{2,1,0:T(8,128)}, u32[]{:S(2)}) copy-start(f32[2,256,256]{2,1,0:T(8,128)} %get-tuple-element.114) | copy-start | bytes 1572868 | tf_op jit(solution)/shard_map/while
  365.6 43.2 %copy-start.1 = (f32[2,256,256]{2,1,0:T(8,128)S(1)}, f32[2,256,256]{2,1,0:T(8,128)}, u32[]{:S(2)}) copy-start(f32[2,256,256]{2,1,0:T(8,128)} %get-tuple-element.114) | copy-start | bytes 1572868 | tf_op jit(solution)/shard_map/while
  411.1 40.2 %copy-start.1 = (f32[2,256,256]{2,1,0:T(8,128)S(1)}, f32[2,256,256]{2,1,0:T(8,128)}, u32[]{:S(2)}) copy-start(f32[2,256,256]{2,1,0:T(8,128)} %get-tuple-element.114) | copy-start | bytes 1572868 | tf_op jit(solution)/shard_map/while
  453.7 43.2 %copy-start.1 = (f32[2,256,256]{2,1,0:T(8,128)S(1)}, f32[2,256,256]{2,1,0:T(8,128)}, u32[]{:S(2)}) copy-start(f32[2,256,256]{2,1,0:T(8,128)} %get-tuple-element.114) | copy-start | bytes 1572868 | tf_op jit(solution)/shard_map/while
  499.3 40.2 %copy-start.1 = (f32[2,256,256]{2,1,0:T(8,128)S(1)}, f32[2,256,256]{2,1,0:T(8,128)}, u32[]{:S(2)}) copy-start(f32[2,256,256]{2,1,0:T(8,128)} %get-tuple-element.114) | copy-start | bytes 1572868 | tf_op jit(solution)/shard_map/while
  541.8 43.2 %copy-start.1 = (f32[2,256,256]{2,1,0:T(8,128)S(1)}, f32[2,256,256]{2,1,0:T(8,128)}, u32[]{:S(2)}) copy-start(f32[2,256,256]{2,1,0:T(8,128)} %get-tuple-element.114) | copy-start | bytes 1572868 | tf_op jit(solution)/shard_map/while
  587.4 40.2 %copy-start.1 = (f32[2,256,256]{2,1,0:T(8,128)S(1)}, f32[2,256,256]{2,1,0:T(8,128)}, u32[]{:S(2)}) copy-start(f32[2,256,256]{2,1,0:T(8,128)} %get-tuple-element.114) | copy-start | bytes 1572868 | tf_op jit(solution)/shard_map/while
  629.9 43.2 %copy-start.1 = (f32[2,256,256]{2,1,0:T(8,128)S(1)}, f32[2,256,256]{2,1,0:T(8,128)}, u32[]{:S(2)}) copy-start(f32[2,256,256]{2,1,0:T(8,128)} %get-tuple-element.114) | copy-start | bytes 1572868 | tf_op jit(solution)/shard_map/while
  675.5 40.2 %copy-start.1 = (f32[2,256,256]{2,1,0:T(8,128)S(1)}, f32[2,256,256]{2,1,0:T(8,128)}, u32[]{:S(2)}) copy-start(f32[2,256,256]{2,1,0:T(8,128)} %get-tuple-element.114) | copy-start | bytes 1572868 | tf_op jit(solution)/shard_map/while
  718.1 43.2 %copy-start.1 = (f32[2,256,256]{2,1,0:T(8,128)S(1)}, f32[2,256,256]{2,1,0:T(8,128)}, u32[]{:S(2)}) copy-start(f32[2,256,256]{2,1,0:T(8,128)} %get-tuple-element.114) | copy-start | bytes 1572868 | tf_op jit(solution)/shard_map/while
  763.6 40.2 %copy-start.1 = (f32[2,256,256]{2,1,0:T(8,128)S(1)}, f32[2,256,256]{2,1,0:T(8,128)}, u32[]{:S(2)}) copy-start(f32[2,256,256]{2,1,0:T(8,128)} %get-tuple-element.114) | copy-start | bytes 1572868 | tf_op jit(solution)/shard_map/while
  806.2 43.2 %copy-start.1 = (f32[2,256,256]{2,1,0:T(8,128)S(1)}, f32[2,256,256]{2,1,0:T(8,128)}, u32[]{:S(2)}) copy-start(f32[2,256,256]{2,1,0:T(8,128)} %get-tuple-element.114) | copy-start | bytes 1572868 | tf_op jit(solution)/shard_map/while
  851.7 40.2 %copy-start.1 = (f32[2,256,256]{2,1,0:T(8,128)S(1)}, f32[2,256,256]{2,1,0:T(8,128)}, u32[]{:S(2)}) copy-start(f32[2,256,256]{2,1,0:T(8,128)} %get-tuple-element.114) | copy-start | bytes 1572868 | tf_op jit(solution)/shard_map/while
  894.3 43.2 %copy-start.1 = (f32[2,256,256]{2,1,0:T(8,128)S(1)}, f32[2,256,256]{2,1,0:T(8,128)}, u32[]{:S(2)}) copy-start(f32[2,256,256]{2,1,0:T(8,128)} %get-tuple-element.114) | copy-start | bytes 1572868 | tf_op jit(solution)/shard_map/while
  939.9 40.2 %copy-start.1 = (f32[2,256,256]{2,1,0:T(8,128)S(1)}, f32[2,256,256]{2,1,0:T(8,128)}, u32[]{:S(2)}) copy-start(f32[2,256,256]{2,1,0:T(8,128)} %get-tuple-element.114) | copy-start | bytes 1572868 | tf_op jit(solution)/shard_map/while
  982.4 43.2 %copy-start.1 = (f32[2,256,256]{2,1,0:T(8,128)S(1)}, f32[2,256,256]{2,1,0:T(8,128)}, u32[]{:S(2)}) copy-start(f32[2,256,256]{2,1,0:T(8,128)} %get-tuple-element.114) | copy-start | bytes 1572868 | tf_op jit(solution)/shard_map/while
  1028.0 40.2 %copy-start.1 = (f32[2,256,256]{2,1,0:T(8,128)S(1)}, f32[2,256,256]{2,1,0:T(8,128)}, u32[]{:S(2)}) copy-start(f32[2,256,256]{2,1,0:T(8,128)} %get-tuple-element.114) | copy-start | bytes 1572868 | tf_op jit(solution)/shard_map/while
  1071.5 1.0 copy-start.2
  1073.7 15.9 %all-to-all-start.3 = ((f32[32,1,512]{2,1,0:T(1,128)}), f32[32,1,512]{2,1,0:T(1,128)S(1)}, u32[]{:S(2)}, u32[]{:S(2)}) async-start(f32[32,1,512]{2,1,0:T(1,128)} %reshape.24), calls=%async_computation.3 | async-start | bytes 131072 | tf_op jit(solution)/shard_map/all_to_all | solution.py:46
  1089.6 56.3 %all-to-all-start.1 = ((f32[32,1,512]{2,1,0:T(1,128)}), f32[32,1,512]{2,1,0:T(1,128)S(1)}, u32[]{:S(2)}, u32[]{:S(2)}) async-start(f32[32,1,512]{2,1,0:T(1,128)} %reshape.28), calls=%async_computation.1 | async-start | bytes 131072 | tf_op jit(solution)/shard_map/all_to_all | solution.py:45
  1145.9 25.0 %all-to-all-start.2 = ((f32[32,1,512]{2,1,0:T(1,128)}), f32[32,1,512]{2,1,0:T(1,128)S(1)}, u32[]{:S(2)}, u32[]{:S(2)}) async-start(f32[32,1,512]{2,1,0:T(1,128)} %reshape.22), calls=%async_computation.2 | async-start | bytes 131072 | tf_op jit(solution)/shard_map/all_to_all | solution.py:44
  1162.4 1.0 copy-start.3
  1170.9 13.8 %all-to-all-start = ((f32[32,1,512]{2,1,0:T(1,128)}), f32[32,1,512]{2,1,0:T(1,128)S(1)}, u32[]{:S(2)}, u32[]{:S(2)}) async-start(f32[32,1,512]{2,1,0:T(1,128)} %reshape.26), calls=%async_computation | async-start | bytes 131072 | tf_op jit(solution)/shard_map/all_to_all | solution.py:43
Sparse Core Ops, SparseCore 0:
  1071.7 72.2 all-reduce.1
where the time goes:
time: 1200 us; the launch traced here: 1190 us
  blocking collectives  984 us (82%)
  matrix products  56.4 us (5%)
  waiting for transfers between devices  44.8 us (4%)
  local copies, waits for them, and re-layouts  44.5 us (4%)
  starting transfers between devices  29.1 us (2%)
  loops' own time  17.9 us (1%)
  between operations  13.7 us (1%)
    all_gather x24, blocking collectives, whole_step(): whole_rows = lax.all_gather(row_block, 'pairs', axis=1, tiled=True)  957 us
    dot_general x24, matrix products, both_sides(): jnp.einsum('pac,picb->iab', row_block, mixed_terms, precision=highest)  30.3 us
    psum x1, blocking collectives, shards(): particle, coupling = lax.psum((particle, coupling), 'aux')  26.1 us
    dot_general x24, matrix products, both_sides(): jnp.einsum('icd,pbd->picb', amps, row_block, precision=highest)  24.8 us
  transfers between devices with their start and end apart: 5, of which 4 were waited for; matrix products, arithmetic and copies ran while one was open for 1% of the time, Pallas kernels for 0%

commit v1 on v0

--- a/solution.py
+++ b/solution.py
@@ -25,7 +25,8 @@
 
     def whole_step(running, block_index):
         row_block = lax.dynamic_slice_in_dim(factors, block_index * 2, 2, 0)
-        whole_rows = lax.all_gather(row_block, "pairs", axis=1, tiled=True)
+        sent = jnp.stack([row_block] * lax.axis_size("pairs"))
+        whole_rows = jnp.concatenate(lax.all_to_all(sent, "pairs", 0, 0), axis=1)
         return (both_sides(running, amplitudes, whole_rows), None)
 
     particle, unused = lax.scan(

time: 1200 us -> 812 us (0.68)
  blocking collectives: 984 us -> 27 us
  waiting for transfers between devices: 44.8 us -> 452 us
  starting transfers between devices: 29.1 us -> 175 us
  local copies, waits for them, and re-layouts: 44.5 us -> 62.7 us
    all_gather x24 -> x0, blocking collectives: 957 us -> none  [whole_step(): whole_rows = lax.all_gather(row_block, 'pairs', axis=1, tiled=True)]
    all_to_all x0 -> x24, waiting for transfers between devices: none -> 408 us  [whole_step(): whole_rows = jnp.concatenate(lax.all_to_all(sent, 'pairs', 0, 0), axis=1)]
    all_to_all x0 -> x24, starting transfers between devices: none -> 147 us  [whole_step(): whole_rows = jnp.concatenate(lax.all_to_all(sent, 'pairs', 0, 0), axis=1)]
    another operation x0 -> x24, local copies, waits for them, and re-layouts: none -> 20.3 us  [whole_step(): sent = jnp.stack([row_block] * lax.axis_size('pairs'))]
  transfers between devices with their start and end apart: 5 -> 29, of which waited for: 4 -> 28; matrix products, arithmetic and copies ran while one was open for 1% -> 1% of each run, Pallas kernels for 0% -> 0%
where the time goes in v1:
time: 812 us; the launch traced here: 805 us
  waiting for transfers between devices  452 us (56%)
  starting transfers between devices  175 us (22%)
  local copies, waits for them, and re-layouts  62.7 us (8%)
  matrix products  56.4 us (7%)
  blocking collectives  27 us (3%)
  loops' own time  14.8 us (2%)
  between operations  13.7 us (2%)
    all_to_all x24, waiting for transfers between devices, whole_step(): whole_rows = jnp.concatenate(lax.all_to_all(sent, 'pairs', 0, 0), axis=1)  408 us
    all_to_all x24, starting transfers between devices, whole_step(): whole_rows = jnp.concatenate(lax.all_to_all(sent, 'pairs', 0, 0), axis=1)  147 us
    dot_general x24, matrix products, both_sides(): jnp.einsum('pac,picb->iab', row_block, mixed_terms, precision=highest)  30.4 us
    psum x1, blocking collectives, shards(): particle, coupling = lax.psum((particle, coupling), 'aux')  27 us
    dot_general x24, matrix products, both_sides(): jnp.einsum('icd,pbd->picb', amps, row_block, precision=highest)  24.8 us
    psum x1, waiting for transfers between devices, shards(): particle, coupling = lax.psum((particle, coupling), 'aux')  21.6 us
    another operation x24, local copies, waits for them, and re-layouts, whole_step(): sent = jnp.stack([row_block] * lax.axis_size('pairs'))  20.3 us
    dynamic_slice x24, local copies, waits for them, and re-layouts, whole_step(): row_block = lax.dynamic_slice_in_dim(factors, block_index * 2, 2, 0)  17.4 us
  transfers between devices with their start and end apart: 29, of which 28 were waited for; matrix products, arithmetic and copies ran while one was open for 1% of the time, Pallas kernels for 0%

profile of v1, /device:TPU:1, one launch (start us, length us, event | category | flops | bytes accessed | tf_op | source)
XLA Modules:
  0.0 805.5 jit_solution(493108633432498514)
XLA Ops:
  6.5 676.2 %while.11 = (s32[]{:T(128)}, f32[2,256,256]{1,2,0:T(8,128)S(1)}, s32[24]{0:T(128)S(1)}, f32[48,8,256]{2,1,0:T(8,128)}, f32[2,256,256]{2,1,0:T(8,128)}, /*index=5*/s32[]{:T(128)}, s32[1]{0:T(128)}, s32[]{:T(128)}, s32[]{:T(128)}) while((s32[]{:T(128)}, f32[2,256,256]{1,2,0:T(8,128)S(1)}, s32[24]{0:T(128)S(1)}, ...), condition=%wide.region_1.2_spmd.clone, body=%wide.region_0.1_spmd.clone.sunk | while | flops 1610874880 | bytes 8962273 | solution.py:32
  9.3 12.9 %all-to-all-start = ((f32[32,2,8,256]{3,2,1,0:T(8,128)}), f32[32,2,8,256]{3,2,1,0:T(8,128)S(1)}, u32[]{:S(2)}, u32[]{:S(2)}) async-start(f32[32,2,8,256]{3,2,1,0:T(8,128)} %stack.4), calls=%async_computation | async-start | bytes 1048576 | tf_op jit(solution)/shard_map/while/body/eval_jaxpr/all_to_all | solution.py:29
  22.2 17.0 %all-to-all-done = f32[32,2,8,256]{3,2,1,0:T(8,128)S(1)} async-done(((f32[32,2,8,256]{3,2,1,0:T(8,128)}), f32[32,2,8,256]{3,2,1,0:T(8,128)S(1)}, u32[]{:S(2)}, u32[]{:S(2)}) %all-to-all-start) | async-done | bytes 524320 | tf_op jit(solution)/shard_map/while/body/eval_jaxpr/all_to_all | solution.py:29
  44.2 5.8 all-to-all-start
  50.0 17.0 %all-to-all-done = f32[32,2,8,256]{3,2,1,0:T(8,128)S(1)} async-done(((f32[32,2,8,256]{3,2,1,0:T(8,128)}), f32[32,2,8,256]{3,2,1,0:T(8,128)S(1)}, u32[]{:S(2)}, u32[]{:S(2)}) %all-to-all-start) | async-done | bytes 524320 | tf_op jit(solution)/shard_map/while/body/eval_jaxpr/all_to_all | solution.py:29
  72.1 5.8 all-to-all-start
  77.9 17.0 %all-to-all-done = f32[32,2,8,256]{3,2,1,0:T(8,128)S(1)} async-done(((f32[32,2,8,256]{3,2,1,0:T(8,128)}), f32[32,2,8,256]{3,2,1,0:T(8,128)S(1)}, u32[]{:S(2)}, u32[]{:S(2)}) %all-to-all-start) | async-done | bytes 524320 | tf_op jit(solution)/shard_map/while/body/eval_jaxpr/all_to_all | solution.py:29
  100.0 5.8 all-to-all-start
  105.8 17.0 %all-to-all-done = f32[32,2,8,256]{3,2,1,0:T(8,128)S(1)} async-done(((f32[32,2,8,256]{3,2,1,0:T(8,128)}), f32[32,2,8,256]{3,2,1,0:T(8,128)S(1)}, u32[]{:S(2)}, u32[]{:S(2)}) %all-to-all-start) | async-done | bytes 524320 | tf_op jit(solution)/shard_map/while/body/eval_jaxpr/all_to_all | solution.py:29
  127.9 5.8 all-to-all-start
  133.7 17.0 %all-to-all-done = f32[32,2,8,256]{3,2,1,0:T(8,128)S(1)} async-done(((f32[32,2,8,256]{3,2,1,0:T(8,128)}), f32[32,2,8,256]{3,2,1,0:T(8,128)S(1)}, u32[]{:S(2)}, u32[]{:S(2)}) %all-to-all-start) | async-done | bytes 524320 | tf_op jit(solution)/shard_map/while/body/eval_jaxpr/all_to_all | solution.py:29
  155.7 5.8 all-to-all-start
  161.6 17.0 %all-to-all-done = f32[32,2,8,256]{3,2,1,0:T(8,128)S(1)} async-done(((f32[32,2,8,256]{3,2,1,0:T(8,128)}), f32[32,2,8,256]{3,2,1,0:T(8,128)S(1)}, u32[]{:S(2)}, u32[]{:S(2)}) %all-to-all-start) | async-done | bytes 524320 | tf_op jit(solution)/shard_map/while/body/eval_jaxpr/all_to_all | solution.py:29
  183.6 5.8 all-to-all-start
  189.5 17.0 %all-to-all-done = f32[32,2,8,256]{3,2,1,0:T(8,128)S(1)} async-done(((f32[32,2,8,256]{3,2,1,0:T(8,128)}), f32[32,2,8,256]{3,2,1,0:T(8,128)S(1)}, u32[]{:S(2)}, u32[]{:S(2)}) %all-to-all-start) | async-done | bytes 524320 | tf_op jit(solution)/shard_map/while/body/eval_jaxpr/all_to_all | solution.py:29
  211.5 5.8 all-to-all-start
  217.3 17.0 %all-to-all-done = f32[32,2,8,256]{3,2,1,0:T(8,128)S(1)} async-done(((f32[32,2,8,256]{3,2,1,0:T(8,128)}), f32[32,2,8,256]{3,2,1,0:T(8,128)S(1)}, u32[]{:S(2)}, u32[]{:S(2)}) %all-to-all-start) | async-done | bytes 524320 | tf_op jit(solution)/shard_map/while/body/eval_jaxpr/all_to_all | solution.py:29
  239.4 5.8 all-to-all-start
  245.2 17.0 %all-to-all-done = f32[32,2,8,256]{3,2,1,0:T(8,128)S(1)} async-done(((f32[32,2,8,256]{3,2,1,0:T(8,128)}), f32[32,2,8,256]{3,2,1,0:T(8,128)S(1)}, u32[]{:S(2)}, u32[]{:S(2)}) %all-to-all-start) | async-done | bytes 524320 | tf_op jit(solution)/shard_map/while/body/eval_jaxpr/all_to_all | solution.py:29
  267.3 5.8 all-to-all-start
  273.1 17.0 %all-to-all-done = f32[32,2,8,256]{3,2,1,0:T(8,128)S(1)} async-done(((f32[32,2,8,256]{3,2,1,0:T(8,128)}), f32[32,2,8,256]{3,2,1,0:T(8,128)S(1)}, u32[]{:S(2)}, u32[]{:S(2)}) %all-to-all-start) | async-done | bytes 524320 | tf_op jit(solution)/shard_map/while/body/eval_jaxpr/all_to_all | solution.py:29
  295.2 5.8 all-to-all-start
  301.0 17.0 %all-to-all-done = f32[32,2,8,256]{3,2,1,0:T(8,128)S(1)} async-done(((f32[32,2,8,256]{3,2,1,0:T(8,128)}), f32[32,2,8,256]{3,2,1,0:T(8,128)S(1)}, u32[]{:S(2)}, u32[]{:S(2)}) %all-to-all-start) | async-done | bytes 524320 | tf_op jit(solution)/shard_map/while/body/eval_jaxpr/all_to_all | solution.py:29
  323.0 5.8 all-to-all-start
  328.9 17.0 %all-to-all-done = f32[32,2,8,256]{3,2,1,0:T(8,128)S(1)} async-done(((f32[32,2,8,256]{3,2,1,0:T(8,128)}), f32[32,2,8,256]{3,2,1,0:T(8,128)S(1)}, u32[]{:S(2)}, u32[]{:S(2)}) %all-to-all-start) | async-done | bytes 524320 | tf_op jit(solution)/shard_map/while/body/eval_jaxpr/all_to_all | solution.py:29
  350.9 5.8 all-to-all-start
  356.7 17.0 %all-to-all-done = f32[32,2,8,256]{3,2,1,0:T(8,128)S(1)} async-done(((f32[32,2,8,256]{3,2,1,0:T(8,128)}), f32[32,2,8,256]{3,2,1,0:T(8,128)S(1)}, u32[]{:S(2)}, u32[]{:S(2)}) %all-to-all-start) | async-done | bytes 524320 | tf_op jit(solution)/shard_map/while/body/eval_jaxpr/all_to_all | solution.py:29
  378.8 5.8 all-to-all-start
  384.6 17.0 %all-to-all-done = f32[32,2,8,256]{3,2,1,0:T(8,128)S(1)} async-done(((f32[32,2,8,256]{3,2,1,0:T(8,128)}), f32[32,2,8,256]{3,2,1,0:T(8,128)S(1)}, u32[]{:S(2)}, u32[]{:S(2)}) %all-to-all-start) | async-done | bytes 524320 | tf_op jit(solution)/shard_map/while/body/eval_jaxpr/all_to_all | solution.py:29
  412.5 17.0 %all-to-all-done = f32[32,2,8,256]{3,2,1,0:T(8,128)S(1)} async-done(((f32[32,2,8,256]{3,2,1,0:T(8,128)}), f32[32,2,8,256]{3,2,1,0:T(8,128)S(1)}, u32[]{:S(2)}, u32[]{:S(2)}) %all-to-all-start) | async-done | bytes 524320 | tf_op jit(solution)/shard_map/while/body/eval_jaxpr/all_to_all | solution.py:29
  434.6 5.8 all-to-all-start
  440.4 17.0 %all-to-all-done = f32[32,2,8,256]{3,2,1,0:T(8,128)S(1)} async-done(((f32[32,2,8,256]{3,2,1,0:T(8,128)}), f32[32,2,8,256]{3,2,1,0:T(8,128)S(1)}, u32[]{:S(2)}, u32[]{:S(2)}) %all-to-all-start) | async-done | bytes 524320 | tf_op jit(solution)/shard_map/while/body/eval_jaxpr/all_to_all | solution.py:29
  468.3 17.0 %all-to-all-done = f32[32,2,8,256]{3,2,1,0:T(8,128)S(1)} async-done(((f32[32,2,8,256]{3,2,1,0:T(8,128)}), f32[32,2,8,256]{3,2,1,0:T(8,128)S(1)}, u32[]{:S(2)}, u32[]{:S(2)}) %all-to-all-start) | async-done | bytes 524320 | tf_op jit(solution)/shard_map/while/body/eval_jaxpr/all_to_all | solution.py:29
  496.2 17.0 %all-to-all-done = f32[32,2,8,256]{3,2,1,0:T(8,128)S(1)} async-done(((f32[32,2,8,256]{3,2,1,0:T(8,128)}), f32[32,2,8,256]{3,2,1,0:T(8,128)S(1)}, u32[]{:S(2)}, u32[]{:S(2)}) %all-to-all-start) | async-done | bytes 524320 | tf_op jit(solution)/shard_map/while/body/eval_jaxpr/all_to_all | solution.py:29
  524.0 17.0 %all-to-all-done = f32[32,2,8,256]{3,2,1,0:T(8,128)S(1)} async-done(((f32[32,2,8,256]{3,2,1,0:T(8,128)}), f32[32,2,8,256]{3,2,1,0:T(8,128)S(1)}, u32[]{:S(2)}, u32[]{:S(2)}) %all-to-all-start) | async-done | bytes 524320 | tf_op jit(solution)/shard_map/while/body/eval_jaxpr/all_to_all | solution.py:29
  546.1 5.8 all-to-all-start
  551.9 17.0 %all-to-all-done = f32[32,2,8,256]{3,2,1,0:T(8,128)S(1)} async-done(((f32[32,2,8,256]{3,2,1,0:T(8,128)}), f32[32,2,8,256]{3,2,1,0:T(8,128)S(1)}, u32[]{:S(2)}, u32[]{:S(2)}) %all-to-all-start) | async-done | bytes 524320 | tf_op jit(solution)/shard_map/while/body/eval_jaxpr/all_to_all | solution.py:29
  579.8 17.0 %all-to-all-done = f32[32,2,8,256]{3,2,1,0:T(8,128)S(1)} async-done(((f32[32,2,8,256]{3,2,1,0:T(8,128)}), f32[32,2,8,256]{3,2,1,0:T(8,128)S(1)}, u32[]{:S(2)}, u32[]{:S(2)}) %all-to-all-start) | async-done | bytes 524320 | tf_op jit(solution)/shard_map/while/body/eval_jaxpr/all_to_all | solution.py:29
  607.7 17.0 %all-to-all-done = f32[32,2,8,256]{3,2,1,0:T(8,128)S(1)} async-done(((f32[32,2,8,256]{3,2,1,0:T(8,128)}), f32[32,2,8,256]{3,2,1,0:T(8,128)S(1)}, u32[]{:S(2)}, u32[]{:S(2)}) %all-to-all-start) | async-done | bytes 524320 | tf_op jit(solution)/shard_map/while/body/eval_jaxpr/all_to_all | solution.py:29
  629.7 5.8 all-to-all-start
  635.6 17.0 %all-to-all-done = f32[32,2,8,256]{3,2,1,0:T(8,128)S(1)} async-done(((f32[32,2,8,256]{3,2,1,0:T(8,128)}), f32[32,2,8,256]{3,2,1,0:T(8,128)S(1)}, u32[]{:S(2)}, u32[]{:S(2)}) %all-to-all-start) | async-done | bytes 524320 | tf_op jit(solution)/shard_map/while/body/eval_jaxpr/all_to_all | solution.py:29
  663.5 17.0 %all-to-all-done = f32[32,2,8,256]{3,2,1,0:T(8,128)S(1)} async-done(((f32[32,2,8,256]{3,2,1,0:T(8,128)}), f32[32,2,8,256]{3,2,1,0:T(8,128)S(1)}, u32[]{:S(2)}, u32[]{:S(2)}) %all-to-all-start) | async-done | bytes 524320 | tf_op jit(solution)/shard_map/while/body/eval_jaxpr/all_to_all | solution.py:29
  693.8 7.6 all-to-all-done.4
  705.4 27.0 %psum.15 = f32[64,64]{1,0:T(8,128)S(1)} all-reduce(f32[64,64]{1,0:T(8,128)S(1)} %reshape.19), channel_id=1, replica_groups=mesh['pairs'=32,'aux'=8] {'aux'}, use_global_device_ids=true, to_apply=%region_3.4 | all-reduce | flops 4096 | bytes 32768 | tf_op jit(solution)/shard_map/psum | solution.py:40
  734.2 21.6 %all-reduce.2.cloned.1.call-done = f32[2,256,256]{2,0,1:T(2,128)} async-done(((f32[2,256,256]{2,0,1:T(2,128)}), f32[2,256,256]{2,0,1:T(2,128)}) %all-reduce.2.cloned.1.call-update) | async-done | bytes 524304 | tf_op jit(solution)/shard_map/psum | solution.py:40
  757.8 15.2 %all-to-all-start.3 = ((f32[32,1,512]{2,1,0:T(1,128)}), f32[32,1,512]{2,1,0:T(1,128)S(1)}, u32[]{:S(2)}, u32[]{:S(2)}) async-start(f32[32,1,512]{2,1,0:T(1,128)} %reshape.32), calls=%async_computation.3 | async-start | bytes 131072 | tf_op jit(solution)/shard_map/all_to_all | solution.py:45
  776.6 6.2 all-to-all-done.3
  788.6 8.0 all-to-all-done.1
  (232 shorter events, 177.4 us)
Async XLA Ops:
  6.5 685.1 %copy-start = (f32[48,8,8]{0,2,1:T(8,128)S(1)}, f32[48,8,8]{0,2,1:T(8,128)}, u32[]{:S(2)}) copy-start(f32[48,8,8]{0,2,1:T(8,128)} %param.7) | copy-start | bytes 36868
  6.5 749.3 %all-reduce.2.cloned.1.call-start = ((), (), s32[]{:S(2)}) async-start(), calls=%async_computation.5 | async-start | bytes 1048576 | tf_op jit(solution)/shard_map/psum | solution.py:40
  9.3 29.9 %copy-start.1 = (f32[2,256,256]{2,1,0:T(8,128)S(1)}, f32[2,256,256]{2,1,0:T(8,128)}, u32[]{:S(2)}) copy-start(f32[2,256,256]{2,1,0:T(8,128)} %get-tuple-element.114) | copy-start | bytes 1572868 | tf_op jit(solution)/shard_map/while
  9.3 29.9 %all-to-all-start = ((f32[32,2,8,256]{3,2,1,0:T(8,128)}), f32[32,2,8,256]{3,2,1,0:T(8,128)S(1)}, u32[]{:S(2)}, u32[]{:S(2)}) async-start(f32[32,2,8,256]{3,2,1,0:T(8,128)} %stack.4), calls=%async_computation | async-start | bytes 1048576 | tf_op jit(solution)/shard_map/while/body/eval_jaxpr/all_to_all | solution.py:29
  44.2 22.8 %copy-start.1 = (f32[2,256,256]{2,1,0:T(8,128)S(1)}, f32[2,256,256]{2,1,0:T(8,128)}, u32[]{:S(2)}) copy-start(f32[2,256,256]{2,1,0:T(8,128)} %get-tuple-element.114) | copy-start | bytes 1572868 | tf_op jit(solution)/shard_map/while
  44.2 22.8 %all-to-all-start = ((f32[32,2,8,256]{3,2,1,0:T(8,128)}), f32[32,2,8,256]{3,2,1,0:T(8,128)S(1)}, u32[]{:S(2)}, u32[]{:S(2)}) async-start(f32[32,2,8,256]{3,2,1,0:T(8,128)} %stack.4), calls=%async_computation | async-start | bytes 1048576 | tf_op jit(solution)/shard_map/while/body/eval_jaxpr/all_to_all | solution.py:29
  72.1 22.8 %copy-start.1 = (f32[2,256,256]{2,1,0:T(8,128)S(1)}, f32[2,256,256]{2,1,0:T(8,128)}, u32[]{:S(2)}) copy-start(f32[2,256,256]{2,1,0:T(8,128)} %get-tuple-element.114) | copy-start | bytes 1572868 | tf_op jit(solution)/shard_map/while
  72.1 22.8 %all-to-all-start = ((f32[32,2,8,256]{3,2,1,0:T(8,128)}), f32[32,2,8,256]{3,2,1,0:T(8,128)S(1)}, u32[]{:S(2)}, u32[]{:S(2)}) async-start(f32[32,2,8,256]{3,2,1,0:T(8,128)} %stack.4), calls=%async_computation | async-start | bytes 1048576 | tf_op jit(solution)/shard_map/while/body/eval_jaxpr/all_to_all | solution.py:29
  100.0 22.8 %copy-start.1 = (f32[2,256,256]{2,1,0:T(8,128)S(1)}, f32[2,256,256]{2,1,0:T(8,128)}, u32[]{:S(2)}) copy-start(f32[2,256,256]{2,1,0:T(8,128)} %get-tuple-element.114) | copy-start | bytes 1572868 | tf_op jit(solution)/shard_map/while
  100.0 22.8 %all-to-all-start = ((f32[32,2,8,256]{3,2,1,0:T(8,128)}), f32[32,2,8,256]{3,2,1,0:T(8,128)S(1)}, u32[]{:S(2)}, u32[]{:S(2)}) async-start(f32[32,2,8,256]{3,2,1,0:T(8,128)} %stack.4), calls=%async_computation | async-start | bytes 1048576 | tf_op jit(solution)/shard_map/while/body/eval_jaxpr/all_to_all | solution.py:29
  127.9 22.8 %copy-start.1 = (f32[2,256,256]{2,1,0:T(8,128)S(1)}, f32[2,256,256]{2,1,0:T(8,128)}, u32[]{:S(2)}) copy-start(f32[2,256,256]{2,1,0:T(8,128)} %get-tuple-element.114) | copy-start | bytes 1572868 | tf_op jit(solution)/shard_map/while
  127.9 22.8 %all-to-all-start = ((f32[32,2,8,256]{3,2,1,0:T(8,128)}), f32[32,2,8,256]{3,2,1,0:T(8,128)S(1)}, u32[]{:S(2)}, u32[]{:S(2)}) async-start(f32[32,2,8,256]{3,2,1,0:T(8,128)} %stack.4), calls=%async_computation | async-start | bytes 1048576 | tf_op jit(solution)/shard_map/while/body/eval_jaxpr/all_to_all | solution.py:29
  155.7 22.8 %copy-start.1 = (f32[2,256,256]{2,1,0:T(8,128)S(1)}, f32[2,256,256]{2,1,0:T(8,128)}, u32[]{:S(2)}) copy-start(f32[2,256,256]{2,1,0:T(8,128)} %get-tuple-element.114) | copy-start | bytes 1572868 | tf_op jit(solution)/shard_map/while
  155.7 22.8 %all-to-all-start = ((f32[32,2,8,256]{3,2,1,0:T(8,128)}), f32[32,2,8,256]{3,2,1,0:T(8,128)S(1)}, u32[]{:S(2)}, u32[]{:S(2)}) async-start(f32[32,2,8,256]{3,2,1,0:T(8,128)} %stack.4), calls=%async_computation | async-start | bytes 1048576 | tf_op jit(solution)/shard_map/while/body/eval_jaxpr/all_to_all | solution.py:29
  183.6 22.8 %copy-start.1 = (f32[2,256,256]{2,1,0:T(8,128)S(1)}, f32[2,256,256]{2,1,0:T(8,128)}, u32[]{:S(2)}) copy-start(f32[2,256,256]{2,1,0:T(8,128)} %get-tuple-element.114) | copy-start | bytes 1572868 | tf_op jit(solution)/shard_map/while
  183.6 22.8 %all-to-all-start = ((f32[32,2,8,256]{3,2,1,0:T(8,128)}), f32[32,2,8,256]{3,2,1,0:T(8,128)S(1)}, u32[]{:S(2)}, u32[]{:S(2)}) async-start(f32[32,2,8,256]{3,2,1,0:T(8,128)} %stack.4), calls=%async_computation | async-start | bytes 1048576 | tf_op jit(solution)/shard_map/while/body/eval_jaxpr/all_to_all | solution.py:29
  211.5 22.8 %copy-start.1 = (f32[2,256,256]{2,1,0:T(8,128)S(1)}, f32[2,256,256]{2,1,0:T(8,128)}, u32[]{:S(2)}) copy-start(f32[2,256,256]{2,1,0:T(8,128)} %get-tuple-element.114) | copy-start | bytes 1572868 | tf_op jit(solution)/shard_map/while
  211.5 22.8 %all-to-all-start = ((f32[32,2,8,256]{3,2,1,0:T(8,128)}), f32[32,2,8,256]{3,2,1,0:T(8,128)S(1)}, u32[]{:S(2)}, u32[]{:S(2)}) async-start(f32[32,2,8,256]{3,2,1,0:T(8,128)} %stack.4), calls=%async_computation | async-start | bytes 1048576 | tf_op jit(solution)/shard_map/while/body/eval_jaxpr/all_to_all | solution.py:29
  239.4 22.8 %copy-start.1 = (f32[2,256,256]{2,1,0:T(8,128)S(1)}, f32[2,256,256]{2,1,0:T(8,128)}, u32[]{:S(2)}) copy-start(f32[2,256,256]{2,1,0:T(8,128)} %get-tuple-element.114) | copy-start | bytes 1572868 | tf_op jit(solution)/shard_map/while
  239.4 22.8 %all-to-all-start = ((f32[32,2,8,256]{3,2,1,0:T(8,128)}), f32[32,2,8,256]{3,2,1,0:T(8,128)S(1)}, u32[]{:S(2)}, u32[]{:S(2)}) async-start(f32[32,2,8,256]{3,2,1,0:T(8,128)} %stack.4), calls=%async_computation | async-start | bytes 1048576 | tf_op jit(solution)/shard_map/while/body/eval_jaxpr/all_to_all | solution.py:29
  267.3 22.8 %all-to-all-start = ((f32[32,2,8,256]{3,2,1,0:T(8,128)}), f32[32,2,8,256]{3,2,1,0:T(8,128)S(1)}, u32[]{:S(2)}, u32[]{:S(2)}) async-start(f32[32,2,8,256]{3,2,1,0:T(8,128)} %stack.4), calls=%async_computation | async-start | bytes 1048576 | tf_op jit(solution)/shard_map/while/body/eval_jaxpr/all_to_all | solution.py:29
  295.2 22.8 %all-to-all-start = ((f32[32,2,8,256]{3,2,1,0:T(8,128)}), f32[32,2,8,256]{3,2,1,0:T(8,128)S(1)}, u32[]{:S(2)}, u32[]{:S(2)}) async-start(f32[32,2,8,256]{3,2,1,0:T(8,128)} %stack.4), calls=%async_computation | async-start | bytes 1048576 | tf_op jit(solution)/shard_map/while/body/eval_jaxpr/all_to_all | solution.py:29
  323.0 22.8 %copy-start.1 = (f32[2,256,256]{2,1,0:T(8,128)S(1)}, f32[2,256,256]{2,1,0:T(8,128)}, u32[]{:S(2)}) copy-start(f32[2,256,256]{2,1,0:T(8,128)} %get-tuple-element.114) | copy-start | bytes 1572868 | tf_op jit(solution)/shard_map/while
  323.0 22.8 %all-to-all-start = ((f32[32,2,8,256]{3,2,1,0:T(8,128)}), f32[32,2,8,256]{3,2,1,0:T(8,128)S(1)}, u32[]{:S(2)}, u32[]{:S(2)}) async-start(f32[32,2,8,256]{3,2,1,0:T(8,128)} %stack.4), calls=%async_computation | async-start | bytes 1048576 | tf_op jit(solution)/shard_map/while/body/eval_jaxpr/all_to_all | solution.py:29
  350.9 22.8 %copy-start.1 = (f32[2,256,256]{2,1,0:T(8,128)S(1)}, f32[2,256,256]{2,1,0:T(8,128)}, u32[]{:S(2)}) copy-start(f32[2,256,256]{2,1,0:T(8,128)} %get-tuple-element.114) | copy-start | bytes 1572868 | tf_op jit(solution)/shard_map/while
  350.9 22.8 %all-to-all-start = ((f32[32,2,8,256]{3,2,1,0:T(8,128)}), f32[32,2,8,256]{3,2,1,0:T(8,128)S(1)}, u32[]{:S(2)}, u32[]{:S(2)}) async-start(f32[32,2,8,256]{3,2,1,0:T(8,128)} %stack.4), calls=%async_computation | async-start | bytes 1048576 | tf_op jit(solution)/shard_map/while/body/eval_jaxpr/all_to_all | solution.py:29
  378.8 22.8 %all-to-all-start = ((f32[32,2,8,256]{3,2,1,0:T(8,128)}), f32[32,2,8,256]{3,2,1,0:T(8,128)S(1)}, u32[]{:S(2)}, u32[]{:S(2)}) async-start(f32[32,2,8,256]{3,2,1,0:T(8,128)} %stack.4), calls=%async_computation | async-start | bytes 1048576 | tf_op jit(solution)/shard_map/while/body/eval_jaxpr/all_to_all | solution.py:29
  406.7 22.8 %all-to-all-start = ((f32[32,2,8,256]{3,2,1,0:T(8,128)}), f32[32,2,8,256]{3,2,1,0:T(8,128)S(1)}, u32[]{:S(2)}, u32[]{:S(2)}) async-start(f32[32,2,8,256]{3,2,1,0:T(8,128)} %stack.4), calls=%async_computation | async-start | bytes 1048576 | tf_op jit(solution)/shard_map/while/body/eval_jaxpr/all_to_all | solution.py:29
  434.6 22.8 %copy-start.1 = (f32[2,256,256]{2,1,0:T(8,128)S(1)}, f32[2,256,256]{2,1,0:T(8,128)}, u32[]{:S(2)}) copy-start(f32[2,256,256]{2,1,0:T(8,128)} %get-tuple-element.114) | copy-start | bytes 1572868 | tf_op jit(solution)/shard_map/while
  434.6 22.8 %all-to-all-start = ((f32[32,2,8,256]{3,2,1,0:T(8,128)}), f32[32,2,8,256]{3,2,1,0:T(8,128)S(1)}, u32[]{:S(2)}, u32[]{:S(2)}) async-start(f32[32,2,8,256]{3,2,1,0:T(8,128)} %stack.4), calls=%async_computation | async-start | bytes 1048576 | tf_op jit(solution)/shard_map/while/body/eval_jaxpr/all_to_all | solution.py:29
  462.4 22.8 %copy-start.1 = (f32[2,256,256]{2,1,0:T(8,128)S(1)}, f32[2,256,256]{2,1,0:T(8,128)}, u32[]{:S(2)}) copy-start(f32[2,256,256]{2,1,0:T(8,128)} %get-tuple-element.114) | copy-start | bytes 1572868 | tf_op jit(solution)/shard_map/while
  462.5 22.8 %all-to-all-start = ((f32[32,2,8,256]{3,2,1,0:T(8,128)}), f32[32,2,8,256]{3,2,1,0:T(8,128)S(1)}, u32[]{:S(2)}, u32[]{:S(2)}) async-start(f32[32,2,8,256]{3,2,1,0:T(8,128)} %stack.4), calls=%async_computation | async-start | bytes 1048576 | tf_op jit(solution)/shard_map/while/body/eval_jaxpr/all_to_all | solution.py:29
  490.3 22.8 %all-to-all-start = ((f32[32,2,8,256]{3,2,1,0:T(8,128)}), f32[32,2,8,256]{3,2,1,0:T(8,128)S(1)}, u32[]{:S(2)}, u32[]{:S(2)}) async-start(f32[32,2,8,256]{3,2,1,0:T(8,128)} %stack.4), calls=%async_computation | async-start | bytes 1048576 | tf_op jit(solution)/shard_map/while/body/eval_jaxpr/all_to_all | solution.py:29
  518.2 22.8 %copy-start.1 = (f32[2,256,256]{2,1,0:T(8,128)S(1)}, f32[2,256,256]{2,1,0:T(8,128)}, u32[]{:S(2)}) copy-start(f32[2,256,256]{2,1,0:T(8,128)} %get-tuple-element.114) | copy-start | bytes 1572868 | tf_op jit(solution)/shard_map/while
  518.2 22.8 %all-to-all-start = ((f32[32,2,8,256]{3,2,1,0:T(8,128)}), f32[32,2,8,256]{3,2,1,0:T(8,128)S(1)}, u32[]{:S(2)}, u32[]{:S(2)}) async-start(f32[32,2,8,256]{3,2,1,0:T(8,128)} %stack.4), calls=%async_computation | async-start | bytes 1048576 | tf_op jit(solution)/shard_map/while/body/eval_jaxpr/all_to_all | solution.py:29
  546.1 22.8 %copy-start.1 = (f32[2,256,256]{2,1,0:T(8,128)S(1)}, f32[2,256,256]{2,1,0:T(8,128)}, u32[]{:S(2)}) copy-start(f32[2,256,256]{2,1,0:T(8,128)} %get-tuple-element.114) | copy-start | bytes 1572868 | tf_op jit(solution)/shard_map/while
  546.1 22.8 %all-to-all-start = ((f32[32,2,8,256]{3,2,1,0:T(8,128)}), f32[32,2,8,256]{3,2,1,0:T(8,128)S(1)}, u32[]{:S(2)}, u32[]{:S(2)}) async-start(f32[32,2,8,256]{3,2,1,0:T(8,128)} %stack.4), calls=%async_computation | async-start | bytes 1048576 | tf_op jit(solution)/shard_map/while/body/eval_jaxpr/all_to_all | solution.py:29
  574.0 22.8 %copy-start.1 = (f32[2,256,256]{2,1,0:T(8,128)S(1)}, f32[2,256,256]{2,1,0:T(8,128)}, u32[]{:S(2)}) copy-start(f32[2,256,256]{2,1,0:T(8,128)} %get-tuple-element.114) | copy-start | bytes 1572868 | tf_op jit(solution)/shard_map/while
  574.0 22.8 %all-to-all-start = ((f32[32,2,8,256]{3,2,1,0:T(8,128)}), f32[32,2,8,256]{3,2,1,0:T(8,128)S(1)}, u32[]{:S(2)}, u32[]{:S(2)}) async-start(f32[32,2,8,256]{3,2,1,0:T(8,128)} %stack.4), calls=%async_computation | async-start | bytes 1048576 | tf_op jit(solution)/shard_map/while/body/eval_jaxpr/all_to_all | solution.py:29
  601.9 22.8 %all-to-all-start = ((f32[32,2,8,256]{3,2,1,0:T(8,128)}), f32[32,2,8,256]{3,2,1,0:T(8,128)S(1)}, u32[]{:S(2)}, u32[]{:S(2)}) async-start(f32[32,2,8,256]{3,2,1,0:T(8,128)} %stack.4), calls=%async_computation | async-start | bytes 1048576 | tf_op jit(solution)/shard_map/while/body/eval_jaxpr/all_to_all | solution.py:29
  629.7 22.8 %copy-start.1 = (f32[2,256,256]{2,1,0:T(8,128)S(1)}, f32[2,256,256]{2,1,0:T(8,128)}, u32[]{:S(2)}) copy-start(f32[2,256,256]{2,1,0:T(8,128)} %get-tuple-element.114) | copy-start | bytes 1572868 | tf_op jit(solution)/shard_map/while
  629.7 22.8 %all-to-all-start = ((f32[32,2,8,256]{3,2,1,0:T(8,128)}), f32[32,2,8,256]{3,2,1,0:T(8,128)S(1)}, u32[]{:S(2)}, u32[]{:S(2)}) async-start(f32[32,2,8,256]{3,2,1,0:T(8,128)} %stack.4), calls=%async_computation | async-start | bytes 1048576 | tf_op jit(solution)/shard_map/while/body/eval_jaxpr/all_to_all | solution.py:29
  657.6 22.8 %copy-start.1 = (f32[2,256,256]{2,1,0:T(8,128)S(1)}, f32[2,256,256]{2,1,0:T(8,128)}, u32[]{:S(2)}) copy-start(f32[2,256,256]{2,1,0:T(8,128)} %get-tuple-element.114) | copy-start | bytes 1572868 | tf_op jit(solution)/shard_map/while
  657.6 22.8 %all-to-all-start = ((f32[32,2,8,256]{3,2,1,0:T(8,128)}), f32[32,2,8,256]{3,2,1,0:T(8,128)S(1)}, u32[]{:S(2)}, u32[]{:S(2)}) async-start(f32[32,2,8,256]{3,2,1,0:T(8,128)} %stack.4), calls=%async_computation | async-start | bytes 1048576 | tf_op jit(solution)/shard_map/while/body/eval_jaxpr/all_to_all | solution.py:29
  685.9 15.5 %all-to-all-start.4 = ((f32[32,1,512]{2,1,0:T(1,128)}), f32[32,1,512]{2,1,0:T(1,128)S(1)}, u32[]{:S(2)}, u32[]{:S(2)}) async-start(f32[32,1,512]{2,1,0:T(1,128)} %reshape.34), calls=%async_computation.4 | async-start | bytes 131072 | tf_op jit(solution)/shard_map/all_to_all | solution.py:47
  701.5 56.3 %all-to-all-start.2 = ((f32[32,1,512]{2,1,0:T(1,128)}), f32[32,1,512]{2,1,0:T(1,128)S(1)}, u32[]{:S(2)}, u32[]{:S(2)}) async-start(f32[32,1,512]{2,1,0:T(1,128)} %reshape.38), calls=%async_computation.2 | async-start | bytes 131072 | tf_op jit(solution)/shard_map/all_to_all | solution.py:46
  757.8 25.0 %all-to-all-start.3 = ((f32[32,1,512]{2,1,0:T(1,128)}), f32[32,1,512]{2,1,0:T(1,128)S(1)}, u32[]{:S(2)}, u32[]{:S(2)}) async-start(f32[32,1,512]{2,1,0:T(1,128)} %reshape.32), calls=%async_computation.3 | async-start | bytes 131072 | tf_op jit(solution)/shard_map/all_to_all | solution.py:45
  782.8 13.8 %all-to-all-start.1 = ((f32[32,1,512]{2,1,0:T(1,128)}), f32[32,1,512]{2,1,0:T(1,128)S(1)}, u32[]{:S(2)}, u32[]{:S(2)}) async-start(f32[32,1,512]{2,1,0:T(1,128)} %reshape.36), calls=%async_computation.1 | async-start | bytes 131072 | tf_op jit(solution)/shard_map/all_to_all | solution.py:44
  (8 other events, 139.1 us)
Sparse Core Ops, SparseCore 0:
  683.9 71.8 all-reduce.1
